TPU v7x, 32 devices: a whole 2x2x4 slice. The times are simulated.
32 devices in a mesh: wide: 8 (over z, x), narrow: 4 (over y, core).
Axes of the slice: x: 2, y: 2, z: 4, core: 2. Of those that a mesh axis runs over, the one named last changes fastest.
Arguments:
- tokens: bfloat16 [24576, 768], P('wide'), may hold values from -6 to 6
- qkv_weight: bfloat16 [3, 768, 768], P(None, None, 'narrow'), may hold values from -0.21875 to 0.21875
- out_weight: bfloat16 [768, 768], P('narrow'), may hold values from -0.875 to 0.875
- norm_bias: float32 [6, 768], replicated, as said below
- up_weight: bfloat16 [2, 768, 3072], P(None, None, 'narrow'), may hold values from -0.21875 to 0.21875
- down_weight: bfloat16 [3072, 768], P('narrow'), may hold values from -0.15625 to 0.15625
- window_lengths: int32 [48], P('wide'), may hold values from 64 to 512, as said below
- cot_out: bfloat16 [24576, 768], P('wide'), may hold values from -6 to 6
Outputs:
- block_out: bfloat16 [24576, 768], P('wide')
- input_grad: float32 [24576, 768], P('wide')
- qkv_grad: float32 [3, 768, 768], P(None, 'wide', 'narrow')
- out_grad: float32 [768, 768], P('narrow', 'wide')
- up_grad: float32 [2, 768, 3072], P(None, 'wide', 'narrow')
- down_grad: float32 [3072, 768], P('narrow', 'wide')
- norm_bias_grad: float32 [6, 768], P(None, 'wide')
Inputs may be any that keep to these rules, and one draw needn't show every extreme that they name: `window_lengths`: keys at or past a window's length are padding; some window holds exactly 512 and some exactly 64. `norm_bias`: rows 0 and 3 lie between 0.5 and 2.
All inputs are finite; a program needn't handle non-finite values.
Results may differ from a plain program's by a relative error of at most 0.025.
Values may be sent and summed in bfloat16 or wider, within the bound.
A program may use at most 192 MiB of HBM per device.

v0:
```python
import math
import jax
import jax.numpy as jnp
from jax import lax
from jax.sharding import PartitionSpec as P

HEADS = 12
HEAD_DIM = 64


def norm_parts(value, gain, shift):
    center = value - jnp.mean(value, axis=-1, keepdims=True)
    spread = jnp.mean(center * center, axis=-1, keepdims=True)
    recip = lax.rsqrt(spread + 1e-05)
    normed = center * recip
    return (normed * gain + shift, normed, recip)


def norm_backward(grad_out, normed, recip, gain):
    scaled = grad_out * gain
    inner = jnp.mean(scaled * normed, axis=-1, keepdims=True)
    grad_in = recip * (scaled - jnp.mean(scaled, axis=-1, keepdims=True) - normed * inner)
    return (grad_in, jnp.sum(grad_out * normed, axis=0), jnp.sum(grad_out, axis=0))


def shards(
    tokens, qkv_weight, out_weight, norm_bias, up_weight, down_weight, window_lengths, cot_out
):
    head_count = qkv_weight.shape[2] // HEAD_DIM
    group_width = qkv_weight.shape[2]
    first_head = lax.axis_index("narrow") * head_count
    slopes = 2.0 ** (-8.0 * (first_head + jnp.arange(head_count) + 1).astype(jnp.float32) / HEADS)
    token_count = tokens.shape[0]
    windows = window_lengths.shape[0]
    window_len = token_count // windows
    score_scale = 1.0 / math.sqrt(HEAD_DIM)
    position = jnp.arange(window_len)
    distance = jnp.abs(position[:, None] - position[None, :]).astype(jnp.float32)

    def score_block(query, key_rows, key_limit):
        raw_scores = jnp.einsum("qhc,khc->hqk", query, key_rows, preferred_element_type=jnp.float32)
        logits = raw_scores * score_scale - slopes[:, None, None] * distance[None]
        return jnp.where(position[None, None, :] < key_limit, logits, -1e30)

    def window_forward(item):
        window_block, key_limit = item
        logits = score_block(window_block[0], window_block[1], key_limit)
        row_top = jnp.max(logits, axis=-1, keepdims=True)
        exponent = jnp.exp(logits - row_top)
        row_total = jnp.sum(exponent, axis=-1, keepdims=True)
        soft_low = (exponent / row_total).astype(jnp.bfloat16)
        log_total = (row_top + jnp.log(row_total))[..., 0]
        result = jnp.einsum(
            "hqk,khc->qhc", soft_low, window_block[2], preferred_element_type=jnp.float32
        )
        return (result.astype(jnp.bfloat16), log_total)

    def window_backward(item):
        window_block, grad_result, log_total, key_limit = item
        logits = score_block(window_block[0], window_block[1], key_limit)
        soft = jnp.exp(logits - log_total[..., None])
        grad_soft = jnp.einsum(
            "qhc,khc->hqk", grad_result, window_block[2], preferred_element_type=jnp.float32
        )
        row_inner = jnp.sum(soft * grad_soft, axis=-1, keepdims=True)
        grad_logit = (soft * (grad_soft - row_inner) * score_scale).astype(jnp.bfloat16)
        grad_query = jnp.einsum(
            "hqk,khc->qhc", grad_logit, window_block[1], preferred_element_type=jnp.float32
        )
        grad_key = jnp.einsum(
            "hqk,qhc->khc", grad_logit, window_block[0], preferred_element_type=jnp.float32
        )
        grad_value = jnp.einsum(
            "hqk,qhc->khc",
            soft.astype(jnp.bfloat16),
            grad_result,
            preferred_element_type=jnp.float32,
        )
        return jnp.stack([grad_query, grad_key, grad_value]).astype(jnp.bfloat16)

    source = tokens.astype(jnp.float32)
    projected = jnp.einsum(
        "td,kdf->ktf", tokens, qkv_weight, preferred_element_type=jnp.float32
    ).astype(jnp.bfloat16)
    window_blocks = jnp.moveaxis(
        projected.reshape(3, windows, window_len, head_count, HEAD_DIM), 1, 0
    )
    attended, log_totals = lax.map(window_forward, (window_blocks, window_lengths))
    attended = attended.reshape(token_count, group_width)
    attn_part = jnp.dot(attended, out_weight, preferred_element_type=jnp.float32)
    attn_branch = lax.psum(attn_part.astype(jnp.bfloat16), "narrow").astype(jnp.float32)
    hidden, normed_one, recip_one = norm_parts(
        attn_branch + norm_bias[2] + source, norm_bias[0], norm_bias[1]
    )
    hidden_low = hidden.astype(jnp.bfloat16)
    gate_up = jnp.einsum("td,kdf->ktf", hidden_low, up_weight, preferred_element_type=jnp.float32)

    def geglu(gate_val, up_val):
        return jax.nn.gelu(gate_val, approximate=False) * up_val

    activation_full, geglu_pull = jax.vjp(geglu, gate_up[0], gate_up[1])
    activation = activation_full.astype(jnp.bfloat16)
    ffn_part = jnp.dot(activation, down_weight, preferred_element_type=jnp.float32)
    ffn_branch = lax.psum(ffn_part.astype(jnp.bfloat16), "narrow").astype(jnp.float32)
    output, normed_two, recip_two = norm_parts(
        ffn_branch + norm_bias[5] + hidden, norm_bias[3], norm_bias[4]
    )
    block_out = output.astype(jnp.bfloat16)
    cotangent = cot_out.astype(jnp.float32)
    grad_second, grad_gain_two, grad_shift_two = norm_backward(
        cotangent, normed_two, recip_two, norm_bias[3]
    )
    grad_down_bias = jnp.sum(grad_second, axis=0)
    grad_second_low = grad_second.astype(jnp.bfloat16)
    down_grad = jnp.einsum(
        "tf,td->fd", activation, grad_second_low, preferred_element_type=jnp.float32
    )
    grad_activation = jnp.einsum(
        "td,fd->tf", grad_second_low, down_weight, preferred_element_type=jnp.float32
    )
    grad_gate, grad_up_val = geglu_pull(grad_activation)
    grad_gate_up = jnp.stack([grad_gate, grad_up_val]).astype(jnp.bfloat16)
    up_grad = jnp.einsum(
        "td,ktf->kdf", hidden_low, grad_gate_up, preferred_element_type=jnp.float32
    )
    hidden_part = jnp.einsum(
        "ktf,kdf->td", grad_gate_up, up_weight, preferred_element_type=jnp.float32
    )
    small_ffn = jnp.stack([grad_gain_two, grad_shift_two, grad_down_bias])
    grad_hidden = grad_second + lax.psum(hidden_part.astype(jnp.bfloat16), "narrow").astype(
        jnp.float32
    )
    grad_first, grad_gain_one, grad_shift_one = norm_backward(
        grad_hidden, normed_one, recip_one, norm_bias[0]
    )
    grad_out_bias = jnp.sum(grad_first, axis=0)
    grad_first_low = grad_first.astype(jnp.bfloat16)
    out_grad = jnp.einsum("tf,td->fd", attended, grad_first_low, preferred_element_type=jnp.float32)
    grad_attended = jnp.einsum(
        "td,fd->tf", grad_first_low, out_weight, preferred_element_type=jnp.float32
    )
    grad_attended = grad_attended.astype(jnp.bfloat16).reshape(
        windows, window_len, head_count, HEAD_DIM
    )
    grad_blocks = lax.map(
        window_backward, (window_blocks, grad_attended, log_totals, window_lengths)
    )
    grad_projected = jnp.moveaxis(grad_blocks, 1, 0).reshape(3, token_count, group_width)
    qkv_grad = jnp.einsum("td,ktf->kdf", tokens, grad_projected, preferred_element_type=jnp.float32)
    source_part = jnp.einsum(
        "ktf,kdf->td", grad_projected, qkv_weight, preferred_element_type=jnp.float32
    )
    small_attn = jnp.stack([grad_gain_one, grad_shift_one, grad_out_bias])
    input_grad = grad_first + lax.psum(source_part.astype(jnp.bfloat16), "narrow").astype(
        jnp.float32
    )
    small_all = jnp.concatenate([small_attn, small_ffn], axis=0)
    qkv_share, out_share, up_share, down_share, small_share = (
        lax.psum_scatter(qkv_grad, "wide", scatter_dimension=1, tiled=True),
        lax.psum_scatter(out_grad, "wide", scatter_dimension=1, tiled=True),
        lax.psum_scatter(up_grad, "wide", scatter_dimension=1, tiled=True),
        lax.psum_scatter(down_grad, "wide", scatter_dimension=1, tiled=True),
        lax.psum_scatter(small_all, "wide", scatter_dimension=1, tiled=True),
    )
    return (block_out, input_grad, qkv_share, out_share, up_share, down_share, small_share)


def solution(mesh):
    placed = (
        P("wide", None),
        P(None, None, "narrow"),
        P("narrow", None),
        P(),
        P(None, None, "narrow"),
        P("narrow", None),
        P("wide"),
        P("wide", None),
    )
    return jax.shard_map(
        shards,
        mesh=mesh,
        in_specs=placed,
        out_specs=(
            P("wide", None),
            P("wide", None),
            P(None, "wide", "narrow"),
            P("narrow", "wide"),
            P(None, "wide", "narrow"),
            P("narrow", "wide"),
            P(None, "wide"),
        ),
        check_vma=False,
    )
```

profile of v0, /device:TPU:0, one launch (start us, length us, event | category | flops | bytes accessed | tf_op | source)
XLA Modules:
  0.0 1051.4 jit_solution(7509393685170289483)
XLA Ops:
  7.2 7.5 fusion.106
  14.7 8.1 reshape.169
  28.1 56.5 %while.24 = (s32[]{:T(128)}, bf16[6,512,3,64]{1,3,2,0:T(8,128)(2,1)}, f32[6,3,512]{2,1,0:T(4,128)}, bf16[6,3,512,3,64]{2,4,3,1,0:T(8,128)(2,1)}, s32[6]{0:T(128)...) while((s32[]{:T(128)}, bf16[6,512,3,64]{1,3,2,0:T(8,128)(2,1)}, ...), condition=%wide.region_3.4_spmd.clone, body=%wide.region_0.3_spmd.clone.sunk | while | flops 210074640 | bytes 24958668 | solution.py:88
  93.0 96.5 %all-reduce.7.cloned.1.call-done = bf16[3072,768]{1,0:T(8,128)(2,1)} async-done(((bf16[3072,768]{1,0:T(8,128)(2,1)}), bf16[3072,768]{1,0:T(8,128)(2,1)}) %all-reduce.7.cloned.1.call-update) | async-done | bytes 4718608 | tf_op jit(solution)/shard_map/psum | solution.py:91
  199.4 11.3 %convolution_bitcast_fusion = f32[2,3072,768]{2,1,0:T(8,128)} fusion(bf16[2,768,768]{2,1,0:T(8,128)(2,1)S(1)} %copy-done, f32[768]{0:T(1024)S(1)} %get-tuple-element.201, f32[768]{0:T(1024)S(1)} %get-tuple-element.202, bf16[3072,768]{1,0:T(8,128)(2,1)S(1)} %bitcast.244, bf16[3072,768]{1,0:T(8,128)(2,1)S(1)} %copy-done.2, f32[3072]{0:T(1024)S(1)} %add_rsqrt_fusion.1, ...), kind=kOutput, calls=%fused_computation.122 | convolution fusion | flops 7268990976 | bytes 30704640 | tf_op jit(solution)/shard_map/td,kdf->ktf/dot_general | solution.py:96
  210.7 22.9 %multiply_convert_fusion.2 = (bf16[3072,768]{1,0:T(8,128)(2,1)S(1)}, f32[3072,768]{1,0:T(8,128)}) fusion(f32[2,3072,768]{2,1,0:T(8,128)} %convolution_bitcast_fusion), kind=kLoop, calls=%fused_computation.100 | loop fusion | flops 155713536 | bytes 33030144 | tf_op jit(solution)/shard_map/convert_element_type | solution.py:102
  241.7 93.8 %all-reduce.9.cloned.1.call-done = bf16[3072,768]{1,0:T(8,128)(2,1)} async-done(((bf16[3072,768]{1,0:T(8,128)(2,1)}), bf16[3072,768]{1,0:T(8,128)(2,1)}) %all-reduce.9.cloned.1.call-update) | async-done | bytes 4718608 | tf_op jit(solution)/shard_map/psum | solution.py:104
  335.5 7.6 fusion.129
  356.8 19.1 %fusion.102 = (bf16[1,3072,768]{2,1,0:T(8,128)(2,1)}, bf16[1,3072,768]{2,1,0:T(8,128)(2,1)}) fusion(f32[3072,768]{1,0:T(8,128)} %get-tuple-element.236, f32[2,3072,768]{2,1,0:T(8,128)} %convolution_bitcast_fusion, bf16[768,768]{1,0:T(8,128)(2,1)} %param.17, f32[3072,768]{1,0:T(8,128)} %get-tuple-element.241), kind=kOutput, calls=%fused_computation.134 | convolution fusion | flops 3668705280 | bytes 48365568 | tf_op jit(solution)/shard_map/td,fd->tf/dot_general | solution.py:118
  376.0 11.6 %bitcast_convert_fusion.1 = bf16[3072,768]{1,0:T(8,128)(2,1)} fusion(bf16[2,768,768]{2,1,0:T(8,128)(2,1)S(1)} %copy-done, bf16[1,3072,768]{2,1,0:T(8,128)(2,1)} %get-tuple-element.240, bf16[1,3072,768]{2,1,0:T(8,128)(2,1)} %get-tuple-element.239), kind=kOutput, calls=%fused_computation.77 | convolution fusion | flops 7254835200 | bytes 16515072 | tf_op jit(solution)/shard_map/ktf,kdf->td/dot_general | solution.py:126
  387.8 94.1 %all-reduce.11.cloned.1.call-done = bf16[3072,768]{1,0:T(8,128)(2,1)} async-done(((bf16[3072,768]{1,0:T(8,128)(2,1)}), bf16[3072,768]{1,0:T(8,128)(2,1)}) %all-reduce.11.cloned.1.call-update) | async-done | bytes 4718608 | tf_op jit(solution)/shard_map/psum | solution.py:130
  481.9 11.2 %multiply_reduce_fusion.1 = (f32[768]{0:T(1024)S(1)}, f32[3072]{0:T(1024)S(1)}, f32[3072]{0:T(1024)S(1)}, f32[768]{0:T(1024)S(1)}, f32[768]{0:T(1024)S(1)}) fusion(f32[3072,768]{1,0:T(8,128)} %get-tuple-element.241, bf16[3072,768]{1,0:T(8,128)(2,1)} %all-reduce.11.cloned.1.call-done, f32[3072]{0:T(1024)S(1)} %add_rsqrt_fusion.1, ...), kind=kLoop, calls=%fused_computation.91 | loop fusion | flops 37740288 | bytes 23657472 | tf_op jit(solution)/shard_map/reduce_sum | solution.py:23
  493.2 12.8 %fusion.128 = (f32[768]{0:T(1024)S(1)}, f32[3072,768]{1,0:T(8,128)}) fusion(f32[3072]{0:T(1024)S(1)} %broadcast_multiply_fusion, f32[3072]{0:T(1024)S(1)} %broadcast_multiply_fusion.5, bf16[3072,768]{1,0:T(8,128)(2,1)} %param.12, f32[768]{0:T(1024)S(1)} %get-tuple-element.203, bf16[3072,768]{1,0:T(8,128)(2,1)} %all-reduce.7.cloned.1.call-done, ...), kind=kLoop, calls=%fused_computation.166 | loop fusion | flops 33029376 | bytes 33088512 | tf_op jit(solution)/shard_map/reduce_sum | solution.py:136
  513.7 17.7 %fusion.116 = f32[2,768,768]{1,2,0:T(8,128)} fusion(bf16[1,3072,768]{2,1,0:T(8,128)(2,1)} %get-tuple-element.240, bf16[1,3072,768]{2,1,0:T(8,128)(2,1)} %get-tuple-element.239, f32[768]{0:T(1024)S(1)} %get-tuple-element.201, f32[768]{0:T(1024)S(1)} %get-tuple-element.202, bf16[3072,768]{1,0:T(8,128)(2,1)} %param.12, ...), kind=kOutput, calls=%fused_computation.145 | convolution fusion | flops 7273709568 | bytes 23626752 | tf_op jit(solution)/shard_map/td,ktf->kdf/dot_general | solution.py:123
  531.4 8.2 copy.46
  549.5 143.8 %while.25 = (s32[]{:T(128)}, bf16[6,3,512,3,64]{2,4,3,1,0:T(8,128)(2,1)}, bf16[6,3,512,3,64]{2,4,3,1,0:T(8,128)(2,1)}, s32[6]{0:T(128)S(1)}, f32[6,3,512]{2,1,0:...) while((s32[]{:T(128)}, ...), condition=%wide.region_17.18_spmd.clone, body=%wide.region_15.17_spmd.clone.sunk | while | flops 518754816 | bytes 39869124 | solution.py:145
  699.9 8.2 reshape.172
  708.1 7.7 bitcast_convert_fusion
  730.1 10.4 fusion.112
  745.0 61.0 %all-reduce.15.cloned.1.call-done = f32[2,768,768]{2,0,1:T(2,128)} async-done(((f32[2,768,768]{2,0,1:T(2,128)}), f32[2,768,768]{2,0,1:T(2,128)}) %all-reduce.15.cloned.1.call-update) | async-done | bytes 4718608
  807.9 93.6 %all-reduce.13.cloned.1.call-done = bf16[3072,768]{1,0:T(8,128)(2,1)} async-done(((bf16[3072,768]{1,0:T(8,128)(2,1)}), bf16[3072,768]{1,0:T(8,128)(2,1)}) %all-reduce.13.cloned.1.call-update) | async-done | bytes 4718608 | tf_op jit(solution)/shard_map/psum | solution.py:154
  901.5 9.7 convert_add_fusion
  911.1 61.2 %reduce-scatter.13.cloned.1.call-done = f32[96,576]{1,0:T(8,128)} async-done(((f32[768,576]{1,0:T(8,128)}), f32[96,576]{1,0:T(8,128)}) %reduce-scatter.13.cloned.1.call-update) | async-done | bytes 221200
  974.2 70.2 %reduce-scatter.11.cloned.1.call-done = f32[768,96]{0,1:T(8,128)} async-done(((f32[768,768]{0,1:T(8,128)}), f32[768,96]{0,1:T(8,128)}) %reduce-scatter.11.cloned.1.call-update) | async-done | bytes 294928 | tf_op jit(solution)/shard_map/reduce_scatter | solution.py:162
  (228 shorter events, 291.3 us)
Async XLA Ops:
  7.2 192.2 %copy-start = (bf16[2,768,768]{2,1,0:T(8,128)(2,1)S(1)}, bf16[2,768,768]{2,1,0:T(8,128)(2,1)}, u32[]{:S(2)}) copy-start(bf16[2,768,768]{2,1,0:T(8,128)(2,1)} %param.16) | copy-start | bytes 7077892
  7.2 182.4 %all-reduce.7.cloned.1.call-start = ((), (), s32[]{:S(2)}) async-start(), calls=%async_computation.4 | async-start | bytes 9437184 | tf_op jit(solution)/shard_map/psum | solution.py:91
  14.7 13.4 %copy-start.12 = (s32[6]{0:T(128)S(1)}, s32[6]{0:T(128)}, u32[]{:S(2)}) copy-start(s32[6]{0:T(128)} %param.18) | copy-start | bytes 76
  86.6 6.4 copy-start.9
  92.7 102.4 %slice-start = ((s8[4718592]{0:T(1024)(128)(4,1)}), s8[524288]{0:T(1024)(128)(4,1)S(1)}, s32[]{:S(2)}) async-start(s8[4718592]{0:T(1024)(128)(4,1)} %bitcast.243), calls=%async_computation.13 | async-start | bytes 1048576
  92.7 242.8 %all-reduce.9.cloned.1.call-start = ((), (), s32[]{:S(2)}) async-start(), calls=%async_computation.5 | async-start | bytes 9437184 | tf_op jit(solution)/shard_map/psum | solution.py:104
  189.6 5.5 copy-start.2
  189.6 6.4 slice-start.1
  210.6 25.0 %copy-start.10 = (bf16[768,768]{1,0:T(8,128)(2,1)S(1)}, bf16[768,768]{1,0:T(8,128)(2,1)}, u32[]{:S(2)}) copy-start(bf16[768,768]{1,0:T(8,128)(2,1)} %param.17) | copy-start | bytes 3538948
  241.1 240.8 %all-reduce.11.cloned.1.call-start = ((), (), s32[]{:S(2)}) async-start(), calls=%async_computation.6 | async-start | bytes 9437184 | tf_op jit(solution)/shard_map/psum | solution.py:130
  343.1 2.3 slice-start.3
  387.6 354.3 %reduce-scatter.17.cloned.1.call-start = ((), (), s32[]{:S(2)}) async-start(), calls=%async_computation.11 | async-start | bytes 442368
  481.9 11.3 %copy-start.4 = (bf16[3072,768]{1,0:T(8,128)(2,1)S(1)}, bf16[3072,768]{1,0:T(8,128)(2,1)}, u32[]{:S(2)}) copy-start(bf16[3072,768]{1,0:T(8,128)(2,1)} %all-reduce.11.cloned.1.call-done) | copy-start | bytes 14155780
  493.2 13.9 %copy-start.6 = (bf16[24,8,6,512]{3,1,2,0:T(8,128)(2,1)S(1)}, bf16[24,8,6,512]{3,1,2,0:T(8,128)(2,1)}, u32[]{:S(2)}) copy-start(bf16[24,8,6,512]{3,1,2,0:T(8,128)(2,1)} %copy-done.5) | copy-start | bytes 3538948
  507.0 236.3 %reduce-scatter.15.cloned.1.call-start = ((), (), s32[]{:S(2)}) async-start(), calls=%async_computation.10 | async-start | bytes 884736
  513.6 292.3 %all-reduce.15.cloned.1.call-start = ((), (), s32[]{:S(2)}) async-start(), calls=%async_computation.12 | async-start | bytes 9437184
  531.4 8.5 copy-start.8
  539.7 9.8 copy-start.13
  539.7 361.8 %all-reduce.13.cloned.1.call-start = ((), (), s32[]{:S(2)}) async-start(), calls=%async_computation.7 | async-start | bytes 9437184 | tf_op jit(solution)/shard_map/psum | solution.py:154
  693.3 14.9 %copy-start.11 = (bf16[3,768,192]{1,2,0:T(8,128)(2,1)S(1)}, bf16[3,768,192]{1,2,0:T(8,128)(2,1)}, u32[]{:S(2)}) copy-start(bf16[3,768,192]{1,2,0:T(8,128)(2,1)} %param.13) | copy-start | bytes 2654212
  715.9 256.4 %reduce-scatter.13.cloned.1.call-start = ((), (), s32[]{:S(2)}) async-start(), calls=%async_computation.9 | async-start | bytes 2211840
  730.1 10.5 %copy-start.14 = (u32[32]{0:T(128)S(1)}, u32[32]{0:T(128)}, u32[]{:S(2)}) copy-start(u32[32]{0:T(128)} %constant.135) | copy-start | bytes 388
  730.1 314.3 %reduce-scatter.11.cloned.1.call-start = ((), (), s32[]{:S(2)}) async-start(), calls=%async_computation.8 | async-start | bytes 2654208 | tf_op jit(solution)/shard_map/reduce_scatter | solution.py:162
  807.1 237.3 %copy-start.1 = (bf16[2,768,768]{2,1,0:T(8,128)(2,1)S(1)}, bf16[2,768,768]{2,1,0:T(8,128)(2,1)}, u32[]{:S(2)}) copy-start(bf16[2,768,768]{2,1,0:T(8,128)(2,1)} %param.16) | copy-start | bytes 7077892
  (9 other events, 15.4 us)
Sparse Core Ops, SparseCore 0:
  92.8 96.7 all-reduce.6
  241.3 94.1 all-reduce.8
  387.7 94.1 all-reduce.10
  507.1 61.5 reduce-scatter.16
  571.9 61.4 reduce-scatter.14
  637.3 168.6 all-reduce.14
  808.4 93.0 all-reduce.12
  905.4 66.9 reduce-scatter.12
  976.4 67.9 reduce-scatter.10
where the time goes:
time: 1060 us; the launch traced here: 1050 us
  waiting for transfers between devices  570 us (54%)
  matrix products  271 us (26%)
  other arithmetic  108 us (10%)
  local copies, waits for them, and re-layouts  84.4 us (8%)
  between operations  15.3 us (1%)
    unnamed x13, waiting for transfers between devices  122 us
    psum x1, waiting for transfers between devices, shards(): lax.psum(attn_part.astype(jnp.bfloat16), 'narrow').astype(jnp.float32)  96.5 us
    psum x1, waiting for transfers between devices, shards(): lax.psum(hidden_part.astype(jnp.bfloat16), 'narrow').astype(jnp.float32)  94.1 us
    psum x1, waiting for transfers between devices, shards(): lax.psum(ffn_part.astype(jnp.bfloat16), 'narrow').astype(jnp.float32)  93.8 us
    psum x1, waiting for transfers between devices, shards(): lax.psum(source_part.astype(jnp.bfloat16), 'narrow').astype(jnp.float32)  93.6 us
    reduce_scatter x1, waiting for transfers between devices, shards(): lax.psum_scatter(down_grad, 'wide', scatter_dimension=1, tiled=True)  70.2 us
    dot_general x6, matrix products, window_backward(): jnp.einsum('hqk,khc->qhc', grad_logit, window_block[1], preferred_element...  34.7 us
    dot_general x6, matrix products, window_backward(): jnp.einsum('hqk,qhc->khc', grad_logit, window_block[0], preferred_element...  34.3 us
  transfers between devices with their start and end apart: 9, of which 7 were waited for; matrix products, arithmetic and copies ran while one was open for 24% of the time, Pallas kernels for 0%

commit v1 on v0

--- a/solution.py
+++ b/solution.py
@@ -88,7 +88,9 @@
     attended, log_totals = lax.map(window_forward, (window_blocks, window_lengths))
     attended = attended.reshape(token_count, group_width)
     attn_part = jnp.dot(attended, out_weight, preferred_element_type=jnp.float32)
-    attn_branch = lax.psum(attn_part.astype(jnp.bfloat16), "narrow").astype(jnp.float32)
+    attn_branch = jnp.sum(lax.all_gather(attn_part.astype(jnp.bfloat16), "narrow"), axis=0).astype(
+        jnp.float32
+    )
     hidden, normed_one, recip_one = norm_parts(
         attn_branch + norm_bias[2] + source, norm_bias[0], norm_bias[1]
     )

time: 1060 us -> 1100 us (1.038)
  waiting for transfers between devices: 570 us -> 593 us
  other arithmetic: 108 us -> 124 us
    all_gather x0 -> x1, waiting for transfers between devices: none -> 121 us  [shards(): lax.all_gather(attn_part.astype(jnp.bfloat16), 'narrow')]
    psum x1 -> x0, waiting for transfers between devices: 96.5 us -> none  [shards(): lax.psum(attn_part.astype(jnp.bfloat16), 'narrow').astype(jnp.float32)]
    reduce_sum x0 -> x1, other arithmetic: none -> 13.5 us  [shards(): jnp.sum(lax.all_gather(attn_part.astype(jnp.bfloat16), 'narrow'), axis=0)]
    unnamed x49 -> x61, local copies, waits for them, and re-layouts: 27.6 us -> 25.8 us
  transfers between devices with their start and end apart: 9 -> 9, of which waited for: 7 -> 7; matrix products, arithmetic and copies ran while one was open for 24% -> 23% of each run, Pallas kernels for 0% -> 0%
where the time goes in v1:
time: 1100 us; the launch traced here: 1090 us
  waiting for transfers between devices  593 us (54%)
  matrix products  271 us (25%)
  other arithmetic  124 us (11%)
  local copies, waits for them, and re-layouts  85.5 us (8%)
  between operations  15.4 us (1%)
    unnamed x13, waiting for transfers between devices  122 us
    all_gather x1, waiting for transfers between devices, shards(): lax.all_gather(attn_part.astype(jnp.bfloat16), 'narrow')  121 us
    psum x1, waiting for transfers between devices, shards(): lax.psum(ffn_part.astype(jnp.bfloat16), 'narrow').astype(jnp.float32)  93.7 us
    psum x1, waiting for transfers between devices, shards(): lax.psum(source_part.astype(jnp.bfloat16), 'narrow').astype(jnp.float32)  93.6 us
    psum x1, waiting for transfers between devices, shards(): lax.psum(hidden_part.astype(jnp.bfloat16), 'narrow').astype(jnp.float32)  92.7 us
    reduce_scatter x1, waiting for transfers between devices, shards(): lax.psum_scatter(down_grad, 'wide', scatter_dimension=1, tiled=True)  70.2 us
    dot_general x6, matrix products, window_backward(): jnp.einsum('hqk,khc->qhc', grad_logit, window_block[1], preferred_element...  34.7 us
    dot_general x6, matrix products, window_backward(): jnp.einsum('hqk,qhc->khc', grad_logit, window_block[0], preferred_element...  34.3 us
  transfers between devices with their start and end apart: 9, of which 7 were waited for; matrix products, arithmetic and copies ran while one was open for 23% of the time, Pallas kernels for 0%

profile of v1, /device:TPU:0, one launch (start us, length us, event | category | flops | bytes accessed | tf_op | source)
XLA Modules:
  0.0 1092.0 jit_solution(4378262494577133079)
XLA Ops:
  14.7 8.1 reshape.169
  28.1 56.5 %while.24 = (s32[]{:T(128)}, bf16[6,512,3,64]{1,3,2,0:T(8,128)(2,1)}, f32[6,3,512]{2,1,0:T(4,128)}, bf16[6,3,512,3,64]{2,4,3,1,0:T(8,128)(2,1)}, s32[6]{0:T(128)...) while((s32[]{:T(128)}, bf16[6,512,3,64]{1,3,2,0:T(8,128)(2,1)}, ...), condition=%wide.region_3.4_spmd.clone, body=%wide.region_0.3_spmd.clone.sunk | while | flops 210074640 | bytes 24958668 | solution.py:88
  93.5 121.0 %all-gather.3.cloned.1.call-done = bf16[12288,768]{1,0:T(8,128)(2,1)} async-done(((bf16[3072,768]{1,0:T(8,128)(2,1)}), bf16[12288,768]{1,0:T(8,128)(2,1)}) %all-gather.3.cloned.1.call-update) | async-done | bytes 18874384 | tf_op jit(solution)/shard_map/all_gather | solution.py:91
  214.5 13.5 %reduce_sum.156 = bf16[3072,768]{1,0:T(8,128)(2,1)} reduce(bf16[4,3072,768]{2,1,0:T(8,128)(2,1)} %bitcast.248, bf16[]{:T(256)} %constant.66.clone.1), dimensions={0}, to_apply=%region_4.5 | reduce | flops 7077888 | bytes 23592962 | tf_op jit(solution)/shard_map/reduce_sum | solution.py:91
  238.8 11.4 %convolution_bitcast_fusion = f32[2,3072,768]{2,1,0:T(8,128)} fusion(bf16[2,768,768]{2,1,0:T(8,128)(2,1)S(1)} %copy-done, f32[768]{0:T(1024)S(1)} %copy-done.12, f32[768]{0:T(1024)S(1)} %copy-done.8, bf16[3072,768]{1,0:T(8,128)(2,1)S(1)} %bitcast.247, bf16[3072,768]{1,0:T(8,128)(2,1)S(1)} %bitcast.245, f32[3072]{0:T(1024)S(1)} %add_rsqrt_fusion.1, ...), kind=kOutput, calls=%fused_computation.122 | convolution fusion | flops 7268990976 | bytes 30704640 | tf_op jit(solution)/shard_map/td,kdf->ktf/dot_general | solution.py:98
  250.2 22.9 %multiply_convert_fusion.2 = (bf16[3072,768]{1,0:T(8,128)(2,1)S(1)}, f32[3072,768]{1,0:T(8,128)}) fusion(f32[2,3072,768]{2,1,0:T(8,128)} %convolution_bitcast_fusion), kind=kLoop, calls=%fused_computation.100 | loop fusion | flops 155713536 | bytes 33030144 | tf_op jit(solution)/shard_map/convert_element_type | solution.py:104
  281.3 93.7 %all-reduce.6.cloned.1.call-done = bf16[3072,768]{1,0:T(8,128)(2,1)} async-done(((bf16[3072,768]{1,0:T(8,128)(2,1)}), bf16[3072,768]{1,0:T(8,128)(2,1)}) %all-reduce.6.cloned.1.call-update) | async-done | bytes 4718608 | tf_op jit(solution)/shard_map/psum | solution.py:106
  374.9 7.8 fusion.129
  397.1 19.1 %fusion.102 = (bf16[1,3072,768]{2,1,0:T(8,128)(2,1)}, bf16[1,3072,768]{2,1,0:T(8,128)(2,1)}) fusion(f32[3072,768]{1,0:T(8,128)} %get-tuple-element.236, f32[2,3072,768]{2,1,0:T(8,128)} %convolution_bitcast_fusion, bf16[768,768]{1,0:T(8,128)(2,1)} %param.17, f32[3072,768]{1,0:T(8,128)} %get-tuple-element.241), kind=kOutput, calls=%fused_computation.134 | convolution fusion | flops 3668705280 | bytes 48365568 | tf_op jit(solution)/shard_map/td,fd->tf/dot_general | solution.py:120
  416.3 11.6 %bitcast_convert_fusion.1 = bf16[3072,768]{1,0:T(8,128)(2,1)} fusion(bf16[2,768,768]{2,1,0:T(8,128)(2,1)S(1)} %copy-done, bf16[1,3072,768]{2,1,0:T(8,128)(2,1)} %get-tuple-element.240, bf16[1,3072,768]{2,1,0:T(8,128)(2,1)} %get-tuple-element.239), kind=kOutput, calls=%fused_computation.77 | convolution fusion | flops 7254835200 | bytes 16515072 | tf_op jit(solution)/shard_map/ktf,kdf->td/dot_general | solution.py:128
  429.5 92.7 %all-reduce.8.cloned.1.call-done = bf16[3072,768]{1,0:T(8,128)(2,1)} async-done(((bf16[3072,768]{1,0:T(8,128)(2,1)}), bf16[3072,768]{1,0:T(8,128)(2,1)}) %all-reduce.8.cloned.1.call-update) | async-done | bytes 4718608 | tf_op jit(solution)/shard_map/psum | solution.py:132
  522.2 11.7 %multiply_reduce_fusion.1 = (f32[768]{0:T(1024)S(1)}, f32[3072]{0:T(1024)S(1)}, f32[3072]{0:T(1024)S(1)}, f32[768]{0:T(1024)S(1)}, f32[768]{0:T(1024)S(1)}) fusion(f32[3072,768]{1,0:T(8,128)} %get-tuple-element.241, bf16[3072,768]{1,0:T(8,128)(2,1)} %all-reduce.8.cloned.1.call-done, f32[3072]{0:T(1024)} %copy-done.6, f32[3072]{0:T(1024)S(1)} %broadcast_multiply_fusion.5, ...), kind=kLoop, calls=%fused_computation.91 | loop fusion | flops 37740288 | bytes 23657472 | tf_op jit(solution)/shard_map/reduce_sum | solution.py:23
  534.0 12.7 %fusion.128 = (f32[768]{0:T(1024)S(1)}, f32[3072,768]{1,0:T(8,128)}) fusion(f32[3072]{0:T(1024)S(1)} %broadcast_multiply_fusion, f32[3072]{0:T(1024)S(1)} %broadcast_multiply_fusion.5, bf16[3072,768]{1,0:T(8,128)(2,1)} %param.12, f32[768]{0:T(1024)S(1)} %get-tuple-element.203, bf16[3072,768]{1,0:T(8,128)(2,1)} %reduce_sum.156, ...), kind=kLoop, calls=%fused_computation.166 | loop fusion | flops 33029376 | bytes 33088512 | tf_op jit(solution)/shard_map/reduce_sum | solution.py:138
  554.4 17.7 %fusion.116 = f32[2,768,768]{1,2,0:T(8,128)} fusion(bf16[1,3072,768]{2,1,0:T(8,128)(2,1)} %get-tuple-element.240, bf16[1,3072,768]{2,1,0:T(8,128)(2,1)} %get-tuple-element.239, f32[768]{0:T(1024)S(1)} %copy-done.13, f32[768]{0:T(1024)S(1)} %copy-done.9, bf16[3072,768]{1,0:T(8,128)(2,1)} %param.12, bf16[3072,768]{1,0:T(8,128)(2,1)} %reduce_sum.156, ...), kind=kOutput, calls=%fused_computation.145 | convolution fusion | flops 7273709568 | bytes 23626752 | tf_op jit(solution)/shard_map/td,ktf->kdf/dot_general | solution.py:125
  572.1 8.2 copy.46
  590.1 143.8 %while.25 = (s32[]{:T(128)}, bf16[6,3,512,3,64]{2,4,3,1,0:T(8,128)(2,1)}, bf16[6,3,512,3,64]{2,4,3,1,0:T(8,128)(2,1)}, s32[6]{0:T(128)S(1)}, f32[6,3,512]{2,1,0:...) while((s32[]{:T(128)}, ...), condition=%wide.region_17.18_spmd.clone, body=%wide.region_15.17_spmd.clone.sunk | while | flops 518754816 | bytes 39869124 | solution.py:147
  740.6 8.2 reshape.172
  748.8 7.7 bitcast_convert_fusion
  770.8 10.4 fusion.112
  785.6 61.0 %all-reduce.12.cloned.1.call-done = f32[2,768,768]{2,0,1:T(2,128)} async-done(((f32[2,768,768]{2,0,1:T(2,128)}), f32[2,768,768]{2,0,1:T(2,128)}) %all-reduce.12.cloned.1.call-update) | async-done | bytes 4718608
  848.6 93.6 %all-reduce.10.cloned.1.call-done = bf16[3072,768]{1,0:T(8,128)(2,1)} async-done(((bf16[3072,768]{1,0:T(8,128)(2,1)}), bf16[3072,768]{1,0:T(8,128)(2,1)}) %all-reduce.10.cloned.1.call-update) | async-done | bytes 4718608 | tf_op jit(solution)/shard_map/psum | solution.py:156
  942.1 9.7 convert_add_fusion
  951.8 61.2 %reduce-scatter.13.cloned.1.call-done = f32[96,576]{1,0:T(8,128)} async-done(((f32[768,576]{1,0:T(8,128)}), f32[96,576]{1,0:T(8,128)}) %reduce-scatter.13.cloned.1.call-update) | async-done | bytes 221200
  1014.9 70.2 %reduce-scatter.11.cloned.1.call-done = f32[768,96]{0,1:T(8,128)} async-done(((f32[768,768]{0,1:T(8,128)}), f32[768,96]{0,1:T(8,128)}) %reduce-scatter.11.cloned.1.call-update) | async-done | bytes 294928 | tf_op jit(solution)/shard_map/reduce_scatter | solution.py:164
  (242 shorter events, 302.2 us)
Async XLA Ops:
  7.2 231.6 %copy-start = (bf16[2,768,768]{2,1,0:T(8,128)(2,1)S(1)}, bf16[2,768,768]{2,1,0:T(8,128)(2,1)}, u32[]{:S(2)}) copy-start(bf16[2,768,768]{2,1,0:T(8,128)(2,1)} %param.16) | copy-start | bytes 7077892
  7.2 207.3 %all-gather.3.cloned.1.call-start = ((), (), s32[]{:S(2)}) async-start(), calls=%async_computation.8 | async-start | bytes 23592960 | tf_op jit(solution)/shard_map/all_gather | solution.py:91
  14.7 13.4 %copy-start.16 = (s32[6]{0:T(128)S(1)}, s32[6]{0:T(128)}, u32[]{:S(2)}) copy-start(s32[6]{0:T(128)} %param.18) | copy-start | bytes 76
  91.7 283.3 %all-reduce.6.cloned.1.call-start = ((), (), s32[]{:S(2)}) async-start(), calls=%async_computation.4 | async-start | bytes 9437184 | tf_op jit(solution)/shard_map/psum | solution.py:106
  228.1 10.7 slice-start.2
  228.1 10.7 copy-start.8
  228.1 10.7 copy-start.12
  238.8 11.5 %copy-start.6 = (f32[3072]{0:T(1024)}, f32[3072]{0:T(1024)S(1)}, u32[]{:S(2)}) copy-start(f32[3072]{0:T(1024)S(1)} %add_rsqrt_fusion.1) | copy-start | bytes 36868
  250.2 25.0 %copy-start.14 = (bf16[768,768]{1,0:T(8,128)(2,1)S(1)}, bf16[768,768]{1,0:T(8,128)(2,1)}, u32[]{:S(2)}) copy-start(bf16[768,768]{1,0:T(8,128)(2,1)} %param.17) | copy-start | bytes 3538948
  280.7 241.5 %all-reduce.8.cloned.1.call-start = ((), (), s32[]{:S(2)}) async-start(), calls=%async_computation.5 | async-start | bytes 9437184 | tf_op jit(solution)/shard_map/psum | solution.py:132
  427.9 354.6 %reduce-scatter.17.cloned.1.call-start = ((), (), s32[]{:S(2)}) async-start(), calls=%async_computation.11 | async-start | bytes 442368
  429.5 104.4 %copy-start.7 = (f32[3072]{0:T(1024)S(1)}, f32[3072]{0:T(1024)}, u32[]{:S(2)}) copy-start(f32[3072]{0:T(1024)} %copy-done.6) | copy-start | bytes 36868
  429.5 104.4 %copy-start.9 = (f32[768]{0:T(1024)S(1)}, f32[768]{0:T(1024)}, u32[]{:S(2)}) copy-start(f32[768]{0:T(1024)} %get-tuple-element.202) | copy-start | bytes 9220
  522.2 11.7 %copy-start.3 = (bf16[3072,768]{1,0:T(8,128)(2,1)S(1)}, bf16[3072,768]{1,0:T(8,128)(2,1)}, u32[]{:S(2)}) copy-start(bf16[3072,768]{1,0:T(8,128)(2,1)} %all-reduce.8.cloned.1.call-done) | copy-start | bytes 14155780
  547.7 236.3 %reduce-scatter.15.cloned.1.call-start = ((), (), s32[]{:S(2)}) async-start(), calls=%async_computation.10 | async-start | bytes 884736
  554.3 292.3 %all-reduce.12.cloned.1.call-start = ((), (), s32[]{:S(2)}) async-start(), calls=%async_computation.12 | async-start | bytes 9437184
  572.1 8.5 copy-start.5
  580.3 9.8 copy-start.17
  580.4 361.8 %all-reduce.10.cloned.1.call-start = ((), (), s32[]{:S(2)}) async-start(), calls=%async_computation.6 | async-start | bytes 9437184 | tf_op jit(solution)/shard_map/psum | solution.py:156
  733.9 14.9 %copy-start.15 = (bf16[3,768,192]{1,2,0:T(8,128)(2,1)S(1)}, bf16[3,768,192]{1,2,0:T(8,128)(2,1)}, u32[]{:S(2)}) copy-start(bf16[3,768,192]{1,2,0:T(8,128)(2,1)} %param.13) | copy-start | bytes 2654212
  756.5 256.5 %reduce-scatter.13.cloned.1.call-start = ((), (), s32[]{:S(2)}) async-start(), calls=%async_computation.9 | async-start | bytes 2211840
  770.7 10.5 copy-start.18
  770.7 314.3 %reduce-scatter.11.cloned.1.call-start = ((), (), s32[]{:S(2)}) async-start(), calls=%async_computation.7 | async-start | bytes 2654208 | tf_op jit(solution)/shard_map/reduce_scatter | solution.py:164
  847.7 237.3 %copy-start.1 = (bf16[2,768,768]{2,1,0:T(8,128)(2,1)S(1)}, bf16[2,768,768]{2,1,0:T(8,128)(2,1)}, u32[]{:S(2)}) copy-start(bf16[2,768,768]{2,1,0:T(8,128)(2,1)} %param.16) | copy-start | bytes 7077892
  (15 other events, 48.2 us)
Sparse Core Ops, SparseCore 0:
  91.8 122.7 all-gather.2
  280.9 94.0 all-reduce.5
  428.0 94.1 all-reduce.7
  547.8 61.5 reduce-scatter.16
  612.5 61.5 reduce-scatter.14
  678.0 168.5 all-reduce.11
  849.1 93.0 all-reduce.9
  946.0 66.9 reduce-scatter.12
  1017.1 67.9 reduce-scatter.10
